TPU v7x, 128 devices: a whole 4x4x4 slice. The times are simulated.
128 devices in a mesh: group: 4 (over x), col: 8 (over y_lo, z), row: 4 (over y_hi, core).
Axes of the slice: x: 4, y: 4 (y_hi: 2, y_lo: 2; y = y_hi * 2 + y_lo), z: 4, core: 2. Of those that a mesh axis runs over, the one named last changes fastest.
Arguments:
- latent: bfloat16 [256, 1024, 320], P('group', ('col', 'row')), may hold values from -6 to 6
- control: bfloat16 [2, 256, 1024, 320], P(None, ('group', 'row'), 'col'), may hold values from -6 to 6
- first_mean: float32 [32], replicated, may hold values from -2 to 2
- first_scale: float32 [32], replicated, may hold values from 0.5 to 2
- first_gain: float32 [320], replicated, may hold values from 0.1 to 1.9
- first_shift: float32 [320], replicated, may hold values from -3 to 3
- first_kernel: bfloat16 [3, 3, 320, 320], replicated, may hold values from -0.109375 to 0.109375
- first_bias: float32 [320], replicated, may hold values from -3 to 3
- branch_mean: float32 [2, 32], replicated, may hold values from -2 to 2
- branch_scale: float32 [2, 32], replicated, may hold values from 0.5 to 2
- branch_gain: float32 [2, 320], replicated, may hold values from 0.1 to 1.9
- branch_shift: float32 [2, 320], replicated, may hold values from -3 to 3
- branch_kernel: bfloat16 [2, 3, 3, 320, 320], replicated, may hold values from -0.109375 to 0.109375
- branch_bias: float32 [2, 320], replicated, may hold values from -3 to 3
- proj_weight: bfloat16 [2, 320, 320], replicated, may hold values from -0.3125 to 0.3125
- proj_bias: float32 [2, 320], replicated, may hold values from -3 to 3
- second_mean: float32 [32], replicated, may hold values from -2 to 2
- second_scale: float32 [32], replicated, may hold values from 0.3 to 1.2
- second_gain: float32 [320], replicated, may hold values from 0.1 to 1.9
- second_shift: float32 [320], replicated, may hold values from -3 to 3
- second_kernel: bfloat16 [3, 3, 320, 320], replicated, may hold values from -0.109375 to 0.109375
- second_bias: float32 [320], replicated, may hold values from -3 to 3
Outputs:
- blended: bfloat16 [256, 1024, 320], P('group', ('col', 'row'))
All inputs are finite; a program needn't handle non-finite values.
Results may differ from a plain program's by a relative error of at most 0.0057.
Values may be sent and summed in bfloat16 or wider, within the bound.
A program may use at most 128 MiB of HBM per device.

v0:
```python
import functools

import jax
import jax.numpy as jnp
from jax import lax
from jax.experimental import pallas as pl
from jax.experimental.pallas import tpu as pltpu
from jax.sharding import PartitionSpec as P

MESH = pl.DeviceIdType.MESH
F32 = jnp.float32
BF16 = jnp.bfloat16
DIRS = [(i, j) for i in (-1, 0, 1) for j in (-1, 0, 1) if (i, j) != (0, 0)]
C = 320
FIRST, BRANCH, SECOND, BIAS = 0, 2, 6, 8
CROWS, CCOLS, CSTRIDE = 16, 128, 144
BROWS, BCOLS, BSTRIDE = 64, 32, 48
PART = 4


def swish(value, table, at):
    half = value * table[at : at + 1, :] + table[at + 1 : at + 2, :]
    return half + half * jnp.tanh(half)


def tiles(value):
    return value[..., 0:128], value[..., 128:256], value[..., 256:320]


class Tiling:
    def __init__(self, mesh_sizes, kind):
        g, c, r = (lax.axis_index(a) for a in ("group", "col", "row"))
        ng, nc, nr = mesh_sizes
        self.nr = nr
        self.kind = kind
        if kind == "branch":
            self.row, self.col, self.rows, self.cols = g * nr + r, c, ng * nr, nc
        else:
            self.row, self.col, self.rows, self.cols = g, c * nr + r, ng, nc * nr

    def at(self, i, j):
        row, col = self.row + i, self.col + j
        if self.kind == "branch":
            return (row // self.nr, col, lax.rem(row, self.nr))
        return (row, col // self.nr, lax.rem(col, self.nr))

    def has(self, i, j):
        row, col = self.row + i, self.col + j
        return (row >= 0) & (row < self.rows) & (col >= 0) & (col < self.cols)


class Halo:
    def __init__(self, tiling, image, rows, cols, bufs):
        self.tiling, self.image, self.rows, self.cols = tiling, image, rows, cols
        self.srow, self.scol, self.scor, self.rrow, self.rcol, self.rcor, self.ss, self.rs = bufs
        self.planes = image.shape[0]
        self.stride = image.shape[2]
        self.flat = image.reshape(self.planes, image.shape[1] * self.stride, 128)

    def slot(self, i, j, bufs):
        row, col, cor = bufs
        if j == 0:
            return row.at[(i + 1) // 2]
        if i == 0:
            return col.at[(j + 1) // 2]
        return cor.at[(i + 1) + (j + 1) // 2]

    def copy(self, i, j):
        n = DIRS.index((i, j))
        return pltpu.make_async_remote_copy(
            src_ref=self.slot(i, j, (self.srow, self.scol, self.scor)),
            dst_ref=self.slot(i, j, (self.rrow, self.rcol, self.rcor)),
            send_sem=self.ss.at[n],
            recv_sem=self.rs.at[n],
            device_id=self.tiling.at(i, j),
            device_id_type=MESH,
        )

    def clear(self):
        for i, j in DIRS:

            @pl.when(jnp.logical_not(self.tiling.has(-i, -j)))
            def _():
                slot = self.slot(i, j, (self.rrow, self.rcol, self.rcor))
                slot[...] = jnp.zeros(slot.shape, slot.dtype)

    def send(self):
        edge_row = {-1: 1, 1: self.rows}
        edge_col = {-1: 8, 1: 7 + self.cols}
        for p in range(self.planes):
            for i in (-1, 1):
                self.srow[(i + 1) // 2, p] = self.image[
                    p, edge_row[i], 8 : 8 + self.cols, :
                ].astype(BF16)
            for j in (-1, 1):
                self.scol[(j + 1) // 2, p] = self.flat[
                    p, pl.ds(self.stride + edge_col[j], self.rows, stride=self.stride), :
                ].astype(BF16)
            for i in (-1, 1):
                for j in (-1, 1):
                    pixel = self.image[p, edge_row[i], edge_col[j] : edge_col[j] + 1, :]
                    self.scor[(i + 1) + (j + 1) // 2, p] = jnp.broadcast_to(
                        pixel, (16, 128)
                    ).astype(BF16)
        for i, j in DIRS:

            @pl.when(self.tiling.has(i, j))
            def _():
                self.copy(i, j).start()

    def receive(self):
        for i, j in DIRS:

            @pl.when(self.tiling.has(-i, -j))
            def _():
                self.copy(i, j).wait_recv()

        halo_row = {1: 0, -1: self.rows + 1}
        halo_col = {1: 7, -1: 8 + self.cols}
        for p in range(self.planes):
            for i in (-1, 1):
                self.image[p, halo_row[i], 8 : 8 + self.cols, :] = self.rrow[
                    (i + 1) // 2, p
                ].astype(F32)
            for j in (-1, 1):
                self.flat[
                    p, pl.ds(self.stride + halo_col[j], self.rows, stride=self.stride), :
                ] = self.rcol[(j + 1) // 2, p].astype(F32)
            for i in (-1, 1):
                for j in (-1, 1):
                    self.image[p, halo_row[i], halo_col[j] : halo_col[j] + 1, :] = self.rcor[
                        (i + 1) + (j + 1) // 2, p
                    ].astype(F32)[0:1]

    def finish(self):
        for i, j in DIRS:

            @pl.when(self.tiling.has(i, j))
            def _():
                self.copy(i, j).wait_send()


def spread(image, plane, row, cols):
    parts = []
    for start in (7, 8, 9):
        for t in range(2):
            parts.append(image[plane + t, row, start : start + cols, :].astype(BF16))
    rest = [
        image[plane + 2, row, start : start + cols, :].astype(BF16)[:, 0:64] for start in (7, 8, 9)
    ]
    parts.append(jnp.concatenate([rest[0], rest[1]], axis=1))
    parts.append(jnp.concatenate([rest[2], jnp.zeros((cols, 64), BF16)], axis=1))
    return jnp.concatenate(parts, axis=1)


def kernel(
    sizes,
    latent_hbm,
    control_hbm,
    table,
    first_hbm,
    branch_hbm,
    second_hbm,
    proj_hbm,
    out_ref,
    latent,
    control,
    main_w,
    rest_w,
    stage_w,
    proj_w,
    cimage,
    bimage,
    cspread,
    bspread,
    crest,
    brest,
    outer,
    send,
    got,
    *more,
):
    halo_bufs = [more[0:8], more[8:16], more[16:24]]
    load_sem, weight_sem, res_send, res_recv = more[24:]
    g, c, r = (lax.axis_index(a) for a in ("group", "col", "row"))
    nr = sizes[2]
    ctile, btile = Tiling(sizes, "branch"), Tiling(sizes, "base")

    barrier = pltpu.get_barrier_semaphore()
    count = nr - 1
    for tile in (ctile, btile):
        for i, j in DIRS:
            there = tile.has(i, j)
            count = count + there.astype(jnp.int32)

            @pl.when(there)
            def _():
                pl.semaphore_signal(
                    barrier, inc=1, device_id=tile.at(i, j), device_id_type=MESH
                )

    def peer(step):
        return (lax.rem(r + 2, 4), lax.rem(r // 2 + 1, 2) * 2 + 1 - lax.rem(r, 2),
                (r // 2) * 2 + 1 - lax.rem(r, 2))[step]

    for step in range(3):
        pl.semaphore_signal(barrier, inc=1, device_id=(g, c, peer(step)), device_id_type=MESH)

    control_load = pltpu.make_async_copy(control_hbm, control, load_sem.at[0])
    control_load.start()
    latent_load = pltpu.make_async_copy(latent_hbm, latent, load_sem.at[1])
    latent_load.start()
    proj_load = pltpu.make_async_copy(proj_hbm, proj_w, load_sem.at[2])
    weight_loads = []
    for n, ref in enumerate(
        (branch_hbm.at[0], branch_hbm.at[1], first_hbm, second_hbm)
    ):
        weight_loads.append(pltpu.make_async_copy(ref, stage_w.at[n], weight_sem.at[n]))
    for load in weight_loads[:2] + [proj_load] + weight_loads[2:]:
        load.start()

    chalo = Halo(ctile, cimage, CROWS, CCOLS, halo_bufs[0])
    bhalo = Halo(btile, bimage, BROWS, BCOLS, halo_bufs[1])
    hhalo = Halo(btile, bimage, BROWS, BCOLS, halo_bufs[2])

    control_load.wait()
    for branch in range(2):

        def act_control(row, _):
            value = swish(
                control[branch, row].astype(F32), table, BRANCH + 2 * branch
            )
            for t, piece in enumerate(tiles(value)):
                cimage[3 * branch + t, row + 1, 8 : 8 + CCOLS, 0 : piece.shape[1]] = piece
            return 0

        lax.fori_loop(0, CROWS, act_control, 0)
    pl.semaphore_wait(barrier, count)
    chalo.send()

    latent_load.wait()

    def act_latent(n, _):
        rows = pl.ds(n * 4, 4)
        value = swish(latent[rows].astype(F32).reshape(4 * BCOLS, C), table, FIRST)
        for t, piece in enumerate(tiles(value)):
            bimage[t, pl.ds(n * 4 + 1, 4), 8 : 8 + BCOLS, 0 : piece.shape[1]] = piece.reshape(
                4, BCOLS, piece.shape[1]
            )
        return 0

    lax.fori_loop(0, BROWS // 4, act_latent, 0)
    bhalo.send()
    chalo.clear()
    bhalo.clear()
    hhalo.clear()

    def arrange(n):
        weight_loads[n].wait()

        def tap_column(dx, _):
            low, high = stage_w.at[n, :, :, 0:256], stage_w.at[n, :, :, 256:320]
            for dy in range(3):
                main_w[n, dy, pl.ds(dx * 256, 256), :] = stage_w[n, dy, dx, 0:256, 0:256]
                main_w[n, dy, pl.ds(768 + dx * 64, 64), :] = stage_w[n, dy, dx, 256:320, 0:256]
            for at, start, size in ((dx * 256, 0, 256), (768 + dx * 64, 256, 64)):
                pieces = [stage_w[n, dy, dx, start : start + size, 256:320] for dy in range(3)]
                rest_w[n, pl.ds(at, size), :] = jnp.concatenate(
                    pieces + [jnp.zeros((size, 64), BF16)], axis=1
                )
            return 0

        lax.fori_loop(0, 3, tap_column, 0)
        for dy in range(3):
            main_w[n, dy, 960:1024, :] = jnp.zeros((64, 256), BF16)
        rest_w[n, 960:1024, :] = jnp.zeros((64, 256), BF16)

    for n in range(4):
        arrange(n)
    proj_load.wait()

    chalo.receive()
    for branch in range(2):

        def spread_control(row, _):
            cspread[branch, row] = spread(cimage, 3 * branch, row, CCOLS)
            return 0

        lax.fori_loop(0, CROWS + 2, spread_control, 0)

        def rest_control(n, _):
            rows = pl.ds(n * 6, 6)
            crest[branch, rows] = jnp.dot(
                cspread[branch, rows].reshape(6 * CCOLS, 1024),
                rest_w[branch],
                preferred_element_type=F32,
            ).reshape(6, CCOLS, 256)
            return 0

        lax.fori_loop(0, 3, rest_control, 0)

    def feature(branch, row):
        wide = jnp.concatenate(
            [
                cspread[branch, pl.ds(row + dy, PART)].reshape(PART * CCOLS, 1024)
                for dy in range(3)
            ],
            axis=1,
        )
        main = jnp.dot(wide, main_w[branch].reshape(3072, 256), preferred_element_type=F32)
        rest = (
            crest[branch, pl.ds(row, PART), :, 0:64]
            + crest[branch, pl.ds(row + 1, PART), :, 64:128]
            + crest[branch, pl.ds(row + 2, PART), :, 128:192]
        ).reshape(PART * CCOLS, 64)
        bias = table[BIAS + branch : BIAS + branch + 1, :]
        return (main + bias[:, 0:256]).astype(BF16), (rest + bias[:, 256:320]).astype(BF16)

    def res_copy(step, part):
        q = peer(step)
        return pltpu.make_async_remote_copy(
            src_ref=send.at[q, pl.ds(part * PART, PART)],
            dst_ref=got.at[pl.ds(r * CROWS + part * PART, PART)],
            send_sem=res_send.at[step, part],
            recv_sem=res_recv.at[step, part],
            device_id=(g, c, q),
            device_id_type=MESH,
        )

    def branch_part(part):
        row = part * PART
        m0, r0 = feature(0, row)
        m1, r1 = feature(1, row)
        both = jnp.concatenate([m0, m1, jnp.concatenate([r0, r1], axis=1)], axis=1)
        proj = jnp.concatenate(
            [
                proj_w[0, 0:256, :],
                proj_w[1, 0:256, :],
                proj_w[0, 256:320, :],
                proj_w[1, 256:320, :],
            ],
            axis=0,
        )
        residual = jnp.dot(both, proj, preferred_element_type=F32) + table[BIAS + 2 : BIAS + 3, :]
        residual = residual.astype(BF16).reshape(PART, CCOLS, C)
        for q in range(4):
            send[q, row : row + PART] = residual[:, q * BCOLS : (q + 1) * BCOLS, :]
        got[pl.ds(r * CROWS + row, PART)] = send[r, row : row + PART]
        for step in range(3):
            res_copy(step, part).start()

    def spread_base(n):
        def one(row, _):
            bspread[row] = spread(bimage, 0, row, BCOLS)
            return 0

        lax.fori_loop(0, BROWS + 2, one, 0)

        def rest(m, _):
            rows = pl.ds(m * 22, 22)
            brest[rows] = jnp.dot(
                bspread[rows].reshape(22 * BCOLS, 1024), rest_w[n], preferred_element_type=F32
            ).reshape(22, BCOLS, 256)
            return 0

        lax.fori_loop(0, 3, rest, 0)

    def conv_base(n, row, bias_at):
        wide = jnp.concatenate(
            [bspread[pl.ds(row + dy, 16)].reshape(16 * BCOLS, 1024) for dy in range(3)], axis=1
        )
        main = jnp.dot(wide, main_w[n].reshape(3072, 256), preferred_element_type=F32)
        rest = (
            brest[pl.ds(row, 16), :, 0:64]
            + brest[pl.ds(row + 1, 16), :, 64:128]
            + brest[pl.ds(row + 2, 16), :, 128:192]
        ).reshape(16 * BCOLS, 64)
        bias = table[bias_at : bias_at + 1, :]
        return jnp.concatenate([main, rest], axis=1) + bias

    branch_part(0)
    branch_part(1)

    bhalo.receive()
    spread_base(2)

    def first_conv(n, _):
        row = n * 16
        value = swish(conv_base(2, row, BIAS + 3), table, SECOND)
        for t, piece in enumerate(tiles(value)):
            bimage[t, pl.ds(row + 1, 16), 8 : 8 + BCOLS, 0 : piece.shape[1]] = piece.reshape(
                16, BCOLS, piece.shape[1]
            )
        return 0

    lax.fori_loop(0, 4, first_conv, 0)
    hhalo.send()

    branch_part(2)
    branch_part(3)

    hhalo.receive()
    spread_base(3)

    def second_conv(n, _):
        row = n * 16
        value = conv_base(3, row, BIAS + 4).reshape(16, BCOLS, C)
        outer[pl.ds(row, 16)] = value + latent[pl.ds(row, 16)].astype(F32)
        return 0

    lax.fori_loop(0, 4, second_conv, 0)

    for step in range(3):
        for part in range(4):
            res_copy(step, part).wait_recv()

    def add_residual(n, _):
        rows = pl.ds(n * 8, 8)
        out_ref[rows] = (outer[rows] + got[rows].astype(F32)).astype(BF16)
        return 0

    lax.fori_loop(0, BROWS // 8, add_residual, 0)
    for step in range(3):
        for part in range(4):
            res_copy(step, part).wait_send()
    for halo in (chalo, bhalo, hhalo):
        halo.finish()


def halo_scratch(planes, rows, cols):
    both = [
        pltpu.VMEM((2, planes, cols, 128), BF16),
        pltpu.VMEM((2, planes, rows, 128), BF16),
        pltpu.VMEM((4, planes, 16, 128), BF16),
    ]
    return both + both + [pltpu.SemaphoreType.DMA((8,)), pltpu.SemaphoreType.DMA((8,))]


def body(
    sizes,
    latent,
    control,
    first_mean,
    first_scale,
    first_gain,
    first_shift,
    first_kernel,
    first_bias,
    branch_mean,
    branch_scale,
    branch_gain,
    branch_shift,
    branch_kernel,
    branch_bias,
    proj_weight,
    proj_bias,
    second_mean,
    second_scale,
    second_gain,
    second_shift,
    second_kernel,
    second_bias,
):
    mean = jnp.concatenate([first_mean[None], branch_mean, second_mean[None]])
    scale = jnp.concatenate([first_scale[None], branch_scale, second_scale[None]])
    gain = jnp.concatenate([first_gain[None], branch_gain, second_gain[None]])
    shift = jnp.concatenate([first_shift[None], branch_shift, second_shift[None]])
    slope = 0.5 * (jnp.repeat(scale, C // scale.shape[1], axis=1) * gain)
    offset = 0.5 * shift - jnp.repeat(mean, C // mean.shape[1], axis=1) * slope
    norms = jnp.stack([slope, offset], axis=1).reshape(8, C)
    table = jnp.concatenate(
        [
            norms,
            branch_bias,
            jnp.sum(proj_bias, axis=0, keepdims=True),
            first_bias[None],
            second_bias[None],
            jnp.zeros((3, C), F32),
        ]
    )
    hbm = pl.BlockSpec(memory_space=pl.ANY)
    vmem = pl.BlockSpec(memory_space=pltpu.VMEM)
    return pl.pallas_call(
        functools.partial(kernel, sizes),
        out_shape=jax.ShapeDtypeStruct((BROWS, BCOLS, C), BF16),
        in_specs=[hbm, hbm, vmem, hbm, hbm, hbm, hbm],
        out_specs=vmem,
        scratch_shapes=[
            pltpu.VMEM((BROWS, BCOLS, C), BF16),
            pltpu.VMEM((2, CROWS, CCOLS, C), BF16),
            pltpu.VMEM((4, 3, 1024, 256), BF16),
            pltpu.VMEM((4, 1024, 256), BF16),
            pltpu.VMEM((4, 3, 3, C, C), BF16),
            pltpu.VMEM((2, C, C), BF16),
            pltpu.VMEM((6, CROWS + 2, CSTRIDE, 128), F32),
            pltpu.VMEM((3, BROWS + 2, BSTRIDE, 128), F32),
            pltpu.VMEM((2, CROWS + 2, CCOLS, 1024), BF16),
            pltpu.VMEM((BROWS + 2, BCOLS, 1024), BF16),
            pltpu.VMEM((2, CROWS + 2, CCOLS, 256), F32),
            pltpu.VMEM((BROWS + 2, BCOLS, 256), F32),
            pltpu.VMEM((BROWS, BCOLS, C), F32),
            pltpu.VMEM((4, CROWS, BCOLS, C), BF16),
            pltpu.VMEM((BROWS, BCOLS, C), BF16),
        ]
        + halo_scratch(6, CROWS, CCOLS)
        + halo_scratch(3, BROWS, BCOLS)
        + halo_scratch(3, BROWS, BCOLS)
        + [
            pltpu.SemaphoreType.DMA((3,)),
            pltpu.SemaphoreType.DMA((4,)),
            pltpu.SemaphoreType.DMA((3, 4)),
            pltpu.SemaphoreType.DMA((3, 4)),
        ],
        compiler_params=pltpu.CompilerParams(
            collective_id=0, has_side_effects=True, vmem_limit_bytes=67_000_000
        ),
    )(latent, control, table, first_kernel, branch_kernel, second_kernel, proj_weight)


def solution(mesh):
    sizes = (mesh.shape["group"], mesh.shape["col"], mesh.shape["row"])
    in_specs = (
        P("group", ("col", "row"), None),
        P(None, ("group", "row"), "col", None),
    ) + (P(),) * 20
    out_specs = P("group", ("col", "row"), None)
    return jax.shard_map(
        functools.partial(body, sizes),
        mesh=mesh,
        in_specs=in_specs,
        out_specs=out_specs,
        check_vma=False,
    )
```

profile of v0, /device:TPU:14, one launch (start us, length us, event | category | flops | bytes accessed | tf_op | source)
XLA Modules:
  0.0 76.9 jit_solution(4233974021101170415)
XLA Ops:
  0.0 0.7 concatenate.46
  0.7 0.7 concatenate.50
  1.4 0.7 broadcast_in_dim.41
  2.0 0.7 concatenate.48
  2.7 0.7 concatenate.52
  3.4 0.7 broadcast_in_dim.42
  4.1 0.7 pad_maximum_fusion.2
  4.8 0.7 pad_maximum_fusion.1
  5.5 0.7 reduce_sum.9
  6.2 0.1 broadcast_in_dim.36
  6.3 0.1 reshape.144
  6.4 0.1 broadcast_in_dim.39
  6.5 0.1 reshape.145
  6.6 0.7 fusion.1
  7.4 1.9 %concatenate.55.table = f32[16,320]{1,0:T(8,128)} concatenate(f32[8,320]{1,0:T(8,128)S(1)} %reshape.146, f32[2,320]{1,0:T(2,128)} %param.35, f32[1,320]{1,0:T(1,128)S(1)} %broadcast_in_dim.40, f32[1,320]{1,0:T(1,128)S(1)} %broadcast_in_dim.41, f32[1,320]{1,0:T(1,128)S(1)} %broadcast_in_dim.42, f32[3,320]{1,0:T(4,128)S(1)} %broadcast_in_dim.43), dimensions={0} | concatenate | bytes 40960 | tf_op jit(solution)/shard_map/concatenate | solution.py:471
  9.3 4.5 %copy.26.control_hbm = bf16[2,16,128,320]{3,2,1,0:T(8,128)(2,1)} copy(bf16[2,16,128,320]{2,3,1,0:T(8,128)(2,1)} %param.23) | data formatting | bytes 5242880 | tf_op args[1]
  13.8 60.3 %shard_map.208 = bf16[64,32,320]{2,1,0:T(8,128)(2,1)} custom-call(bf16[64,32,320]{2,1,0:T(8,128)(2,1)} %latent_hbm.1, bf16[2,16,128,320]{3,2,1,0:T(8,128)(2,1)} %copy.26.control_hbm, f32[16,320]{1,0:T(8,128)} %concatenate.55.table, bf16[3,3,320,320]{3,2,1,0:T(8,128)(2,1)} %first_hbm.1, bf16[2,3,3,320,320]{4,3,2,1,0:T(8,128)(2,1)} %branch_hbm.1, ...), custom_call_target="tpu_custom_call" | custom-call | tf_op jit(solution)/shard_map/pallas_call | solution.py:483
  74.2 2.7 %copy.28 = bf16[64,32,320]{2,1,0:T(8,128)(2,1)} copy(bf16[64,32,320]{2,1,0:T(8,128)(2,1)} %shard_map.208) | data formatting | bytes 2621440
  (5 shorter events, 0.0 us)
where the time goes:
time: 77.4 us; the launch traced here: 76.9 us
  Pallas kernels  60.3 us (78%)
  local copies, waits for them, and re-layouts  13.7 us (18%)
  other arithmetic  2.83 us (4%)
    pallas_call x1, Pallas kernels, body(): pl.pallas_call(functools.partial(kernel, sizes), out_shape=jax.ShapeDtype...  60.3 us
    unnamed x2, local copies, waits for them, and re-layouts  7.25 us
    concatenate x1, local copies, waits for them, and re-layouts, body(): jnp.concatenate([norms, branch_bias, jnp.sum(proj_bias, axis=0, keepdims=...  1.9 us

commit v1 on v0

v1 whole, which is shorter than its diff:
```python
import functools

import jax
import jax.numpy as jnp
from jax import lax
from jax.experimental import pallas as pl
from jax.experimental.pallas import tpu as pltpu
from jax.sharding import PartitionSpec as P

MESH = pl.DeviceIdType.MESH
F32 = jnp.float32
BF16 = jnp.bfloat16
DIRS = [(i, j) for i in (-1, 0, 1) for j in (-1, 0, 1) if (i, j) != (0, 0)]
C = 320
FIRST, BRANCH, SECOND, BIAS = 0, 2, 6, 8
CROWS, CCOLS = 16, 128
BROWS, BCOLS = 64, 32
BLOCK, STRIDE = 128, 144
PART = 4
CHUNK = 16


def swish(value, table, at):
    half = value * table[at : at + 1, :] + table[at + 1 : at + 2, :]
    return half + half * jnp.tanh(half)


def widen(stat):
    groups = stat.shape[1]
    across = lax.broadcasted_iota(jnp.int32, (groups, groups), 0)
    along = lax.broadcasted_iota(jnp.int32, (groups, groups), 1)
    column = jnp.sum(
        jnp.where(across == along, jnp.broadcast_to(stat, (groups, groups)), 0.0),
        axis=1,
        keepdims=True,
    )
    first = lax.broadcasted_iota(jnp.int32, (groups, C), 0) * (C // groups)
    channel = lax.broadcasted_iota(jnp.int32, (groups, C), 1)
    inside = (channel >= first) & (channel < first + C // groups)
    return jnp.sum(
        jnp.where(inside, jnp.broadcast_to(column, (groups, C)), 0.0), axis=0, keepdims=True
    )


class Tiling:
    def __init__(self, mesh_sizes, kind):
        g, c, r = (lax.axis_index(a) for a in ("group", "col", "row"))
        ng, nc, nr = mesh_sizes
        self.nr = nr
        self.kind = kind
        if kind == "branch":
            self.row, self.col, self.rows, self.cols = g * nr + r, c, ng * nr, nc
        else:
            self.row, self.col, self.rows, self.cols = g, c * nr + r, ng, nc * nr

    def at(self, i, j):
        row, col = self.row + i, self.col + j
        if self.kind == "branch":
            return (row // self.nr, col, lax.rem(row, self.nr))
        return (row, col // self.nr, lax.rem(col, self.nr))

    def has(self, i, j):
        row, col = self.row + i, self.col + j
        return (row >= 0) & (row < self.rows) & (col >= 0) & (col < self.cols)


class Halo:
    def __init__(self, tiling, image, rows, cols, bufs):
        self.tiling, self.image, self.rows, self.cols = tiling, image, rows, cols
        self.srow, self.scol, self.scor, self.rrow, self.rcol, self.rcor, self.ss, self.rs = bufs
        self.planes = image.shape[0]
        self.per = BLOCK // cols
        self.blocks = rows // self.per
        self.flat = image.reshape(self.planes, image.shape[1] * STRIDE, 128)

    def slot(self, i, j, bufs):
        row, col, cor = bufs
        if j == 0:
            return row.at[(i + 1) // 2]
        if i == 0:
            return col.at[(j + 1) // 2]
        return cor.at[(i + 1) + (j + 1) // 2]

    def copy(self, i, j):
        n = DIRS.index((i, j))
        return pltpu.make_async_remote_copy(
            src_ref=self.slot(i, j, (self.srow, self.scol, self.scor)),
            dst_ref=self.slot(i, j, (self.rrow, self.rcol, self.rcor)),
            send_sem=self.ss.at[n],
            recv_sem=self.rs.at[n],
            device_id=self.tiling.at(i, j),
            device_id_type=MESH,
        )

    def clear(self):
        for i, j in DIRS:

            @pl.when(jnp.logical_not(self.tiling.has(-i, -j)))
            def _():
                slot = self.slot(i, j, (self.rrow, self.rcol, self.rcor))
                slot[...] = jnp.zeros(slot.shape, slot.dtype)

    def send(self):
        cols, blocks = self.cols, self.blocks
        edge = {-1: (0, 8), 1: (blocks - 1, 8 + BLOCK - cols)}
        for p in range(self.planes):
            for i in (-1, 1):
                block, at = edge[i]
                self.srow[(i + 1) // 2, p] = self.image[p, block, at : at + cols, :].astype(BF16)
                for j in (-1, 1):
                    pixel = at + (cols - 1) * ((j + 1) // 2)
                    self.scor[(i + 1) + (j + 1) // 2, p] = jnp.broadcast_to(
                        self.image[p, block, pixel : pixel + 1, :], (16, 128)
                    ).astype(BF16)
            for j in (-1, 1):
                for inner in range(self.per):
                    start = 8 + inner * cols + (cols - 1) * ((j + 1) // 2)
                    self.scol[(j + 1) // 2, p, inner * blocks : (inner + 1) * blocks] = self.flat[
                        p, pl.ds(start, blocks, stride=STRIDE), :
                    ].astype(BF16)
        for i, j in DIRS:

            @pl.when(self.tiling.has(i, j))
            def _():
                self.copy(i, j).start()

    def receive(self, targets, sides):
        cols, blocks = self.cols, self.blocks
        for i, j in DIRS:

            @pl.when(self.tiling.has(-i, -j))
            def _():
                self.copy(i, j).wait_recv()

        for n, target in enumerate(targets):
            for i in (-1, 1):
                for t in range(3):
                    p = 3 * n + t
                    self.image[p, blocks, 8 : 8 + cols, :] = self.rrow[(i + 1) // 2, p].astype(F32)
                    for j, at in ((1, 7), (-1, 8 + cols)):
                        self.image[p, blocks, at : at + 1, :] = self.rcor[
                            (i + 1) + (j + 1) // 2, p
                        ].astype(F32)[0:1]
                row = 0 if i == 1 else self.rows + 1
                spread(self.image, 3 * n, blocks, cols, target.at[pl.ds(row, 1)])
            for j in (-1, 1):
                for t in range(3):
                    sides[(j + 1) // 2, t, 0 : self.rows // 8] = (
                        self.rcol[(j + 1) // 2, 3 * n + t]
                        .astype(F32)
                        .reshape(self.rows // 8, 8, 128)
                    )
            sub = lax.broadcasted_iota(jnp.int32, (16, 128), 0)
            lane = lax.broadcasted_iota(jnp.int32, (16, 128), 1)
            places = (
                (1, 0, 0, False),
                (1, 1, 128, False),
                (1, 2, 768, True),
                (0, 0, 512, False),
                (0, 1, 640, False),
                (0, 2, 896, True),
            )

            def fix(group, _):
                for s in range(8):
                    k = group * 8 + s
                    row = lax.rem(k, blocks) * self.per + k // blocks + 1
                    for side, t, lanes, leftover in places:
                        edge = (sub == 0) if side == 1 else (sub == 15)
                        if leftover:
                            edge = edge & (lane < 64)
                        at = 0 if side == 1 else cols - 16
                        pixel = jnp.broadcast_to(sides[side, t, group, s : s + 1, :], (16, 128))
                        held = target[row, at : at + 16, lanes : lanes + 128]
                        target[row, at : at + 16, lanes : lanes + 128] = jnp.where(
                            edge, pixel, held.astype(F32)
                        ).astype(BF16)
                return 0

            lax.fori_loop(0, self.rows // 8, fix, 0)

    def finish(self):
        for i, j in DIRS:

            @pl.when(self.tiling.has(i, j))
            def _():
                self.copy(i, j).wait_send()


def place(image, plane, block, value):
    image[plane, block, 8 : 8 + BLOCK, :] = value[:, 0:128]
    image[plane + 1, block, 8 : 8 + BLOCK, :] = value[:, 128:256]
    image[plane + 2, block, 8 : 8 + BLOCK, 0:64] = value[:, 256:320]


def spread(image, plane, block, cols, target):
    rows = target.shape[0]
    size = rows * cols
    rest = []
    for n, start in enumerate((7, 8, 9)):
        for t in range(2):
            piece = image[plane + t, block, start : start + size, :].astype(BF16)
            lanes = n * 256 + t * 128
            target[:, :, lanes : lanes + 128] = piece.reshape(rows, cols, 128)
        rest.append(image[plane + 2, block, start : start + size, :][:, 0:64])
    for lanes, pair in ((768, rest[0:2]), (896, [rest[2], jnp.zeros((size, 64), F32)])):
        piece = jnp.concatenate(pair, axis=1).astype(BF16)
        target[:, :, lanes : lanes + 128] = piece.reshape(rows, cols, 128)


def kernel(
    sizes,
    latent_hbm,
    control_hbm,
    first_hbm,
    branch_hbm,
    second_hbm,
    proj_hbm,
    first_mean,
    first_scale,
    first_gain,
    first_shift,
    first_bias,
    branch_mean,
    branch_scale,
    branch_gain,
    branch_shift,
    branch_bias,
    proj_bias,
    second_mean,
    second_scale,
    second_gain,
    second_shift,
    second_bias,
    out_ref,
    table,
    latent,
    control,
    main_w,
    tail_w,
    rest_w,
    stage_w,
    proj_w,
    cimage,
    bimage,
    cspread,
    bspread,
    hspread,
    crest,
    outer,
    send,
    got,
    sides,
    *more,
):
    halo_bufs = [more[0:8], more[8:16], more[16:24]]
    load_sem, weight_sem, res_send, res_recv = more[24:]
    g, c, r = (lax.axis_index(a) for a in ("group", "col", "row"))
    nr = sizes[2]
    ctile, btile = Tiling(sizes, "branch"), Tiling(sizes, "base")

    control_loads = [
        pltpu.make_async_copy(control_hbm.at[k], control.at[k], load_sem.at[k]) for k in range(2)
    ]
    for load in control_loads:
        load.start()

    barrier = pltpu.get_barrier_semaphore()
    count = nr - 1
    for tile in (ctile, btile):
        for i, j in DIRS:
            there = tile.has(i, j)
            count = count + there.astype(jnp.int32)

            @pl.when(there)
            def _():
                pl.semaphore_signal(
                    barrier, inc=1, device_id=tile.at(i, j), device_id_type=MESH
                )

    def peer(step):
        far = lax.rem(r // 2 + 1, 2) * 2
        core = lax.rem(r, 2)
        return (far + core, far + 1 - core, (r // 2) * 2 + 1 - core)[step]

    for step in range(3):
        pl.semaphore_signal(barrier, inc=1, device_id=(g, c, peer(step)), device_id_type=MESH)

    chalo = Halo(ctile, cimage, CROWS, CCOLS, halo_bufs[0])
    bhalo = Halo(btile, bimage, BROWS, BCOLS, halo_bufs[1])
    hhalo = Halo(btile, bimage, BROWS, BCOLS, halo_bufs[2])

    norms = ((first_mean, first_scale, first_gain, first_shift, 0),) + tuple(
        (branch_mean, branch_scale, branch_gain, branch_shift, k) for k in range(2)
    ) + ((second_mean, second_scale, second_gain, second_shift, 0),)

    def vector(ref, k):
        return ref[...].reshape(1, -1) if len(ref.shape) == 1 else ref[k : k + 1, :]

    for n, (*stats, k) in enumerate(norms):
        mean, scale, gain, shift = (vector(ref, k) for ref in stats)
        slope = 0.5 * (widen(scale) * gain)
        table[2 * n : 2 * n + 1, :] = slope
        table[2 * n + 1 : 2 * n + 2, :] = 0.5 * shift - widen(mean) * slope
    table[BIAS : BIAS + 2, :] = branch_bias[...]
    table[BIAS + 2 : BIAS + 3, :] = proj_bias[0:1, :] + proj_bias[1:2, :]
    table[BIAS + 3 : BIAS + 4, :] = vector(first_bias, 0)
    table[BIAS + 4 : BIAS + 5, :] = vector(second_bias, 0)

    for load in control_loads:
        load.wait()
    latent_load = pltpu.make_async_copy(latent_hbm, latent, load_sem.at[2])
    proj_load = pltpu.make_async_copy(proj_hbm, proj_w, load_sem.at[3])

    def weight_loads(n):
        ref = (branch_hbm.at[0], branch_hbm.at[1], first_hbm, second_hbm)[n]
        return (
            pltpu.make_async_copy(
                ref.at[:, :, 0:256, 0:256], main_w.at[n], weight_sem.at[n, 0]
            ),
            pltpu.make_async_copy(
                ref.at[:, :, 256:320, 0:256], tail_w.at[n, :, 0:3], weight_sem.at[n, 1]
            ),
            pltpu.make_async_copy(ref.at[:, :, :, 256:320], stage_w.at[n], weight_sem.at[n, 2]),
        )

    for load in (
        *weight_loads(0),
        *weight_loads(1),
        proj_load,
        latent_load,
        *weight_loads(2),
        *weight_loads(3),
    ):
        load.start()

    for branch in range(2):

        def act_control(n, _):
            for row in (2 * n, 2 * n + 1):
                value = swish(control[branch, row].T.astype(F32), table, BRANCH + 2 * branch)
                place(cimage, 3 * branch, row, value)
                spread(cimage, 3 * branch, row, CCOLS, cspread.at[branch, pl.ds(row + 1, 1)])
            return 0

        lax.fori_loop(0, CROWS // 2, act_control, 0)
    pl.semaphore_wait(barrier, count)
    chalo.send()
    chalo.clear()
    bhalo.clear()
    hhalo.clear()

    def arrange(n):
        for load in weight_loads(n):
            load.wait()

        def tap_column(dx, _):
            for at, start, size in ((dx * 256, 0, 256), (768 + dx * 64, 256, 64)):
                pieces = [stage_w[n, dy, dx, start : start + size, :] for dy in range(3)]
                rest_w[n, pl.ds(at, size), :] = jnp.concatenate(
                    pieces + [jnp.zeros((size, 64), BF16)], axis=1
                )
            return 0

        lax.fori_loop(0, 3, tap_column, 0)
        for dy in range(3):
            tail_w[n, dy, 3] = jnp.zeros((64, 256), BF16)
        rest_w[n, 960:1024, :] = jnp.zeros((64, 256), BF16)

    def main_dot(image_rows, n):
        weight = []
        for dy in range(3):
            weight += [main_w[n, dy].reshape(768, 256), tail_w[n, dy].reshape(256, 256)]
        return jnp.dot(
            jnp.concatenate(image_rows, axis=1),
            jnp.concatenate(weight, axis=0),
            preferred_element_type=F32,
        )

    def act_latent(n):
        value = swish(
            latent[pl.ds(n * 4, 4)].astype(F32).reshape(BLOCK, C), table, FIRST
        )
        place(bimage, 0, n, value)
        spread(bimage, 0, n, BCOLS, bspread.at[pl.ds(n * 4 + 1, 4)])

    def res_copy(step, part):
        q = peer(step)
        return pltpu.make_async_remote_copy(
            src_ref=send.at[q, part],
            dst_ref=got.at[r * 4 + part],
            send_sem=res_send.at[step, part],
            recv_sem=res_recv.at[step, part],
            device_id=(g, c, q),
            device_id_type=MESH,
        )

    def branch_part(part, beside=()):
        row = part * PART
        first, last = (0, PART + 2) if part == 0 else (row + 2, row + PART + 2)
        features = []
        for branch in range(2):
            for work in beside[branch::2]:
                act_latent(work)
            size = (last - first) * CCOLS
            crest[branch, first:last] = jnp.dot(
                cspread[branch, first:last].reshape(size, 1024),
                rest_w[branch],
                preferred_element_type=F32,
            ).reshape(last - first, CCOLS, 256)
            main = main_dot(
                [
                    cspread[branch, row + dy : row + dy + PART].reshape(PART * CCOLS, 1024)
                    for dy in range(3)
                ],
                branch,
            )
            rest = (
                crest[branch, row : row + PART, :, 0:64]
                + crest[branch, row + 1 : row + 1 + PART, :, 64:128]
                + crest[branch, row + 2 : row + 2 + PART, :, 128:192]
            ).reshape(PART * CCOLS, 64)
            bias = table[BIAS + branch : BIAS + branch + 1, :]
            features.append(
                ((main + bias[:, 0:256]).astype(BF16), (rest + bias[:, 256:320]).astype(BF16))
            )
        (m0, r0), (m1, r1) = features
        both = jnp.concatenate([m0, m1, jnp.concatenate([r0, r1], axis=1)], axis=1)
        proj = jnp.concatenate(
            [
                proj_w[0, 0:256, :],
                proj_w[1, 0:256, :],
                proj_w[0, 256:320, :],
                proj_w[1, 256:320, :],
            ],
            axis=0,
        )
        residual = jnp.dot(both, proj, preferred_element_type=F32) + table[BIAS + 2 : BIAS + 3, :]
        residual = residual.reshape(PART, CCOLS, C)
        for q in range(4):
            block = residual[:, q * BCOLS : (q + 1) * BCOLS, :].reshape(BLOCK, C)
            send[q, part, 0:128] = block[:, 0:128].astype(BF16)
            send[q, part, 128:256] = block[:, 128:256].astype(BF16)
            send[q, part, 256:320] = jnp.concatenate(
                [block[0:64, 256:320], block[64:128, 256:320]], axis=1
            ).astype(BF16)
        for step in range(3):
            res_copy(step, part).start()
        got[r * 4 + part] = send[r, part]

    def conv_base(n, image, row, bias_at):
        main = main_dot(
            [image[row + dy : row + dy + CHUNK].reshape(CHUNK * BCOLS, 1024) for dy in range(3)],
            n,
        )
        every = jnp.dot(
            image[row : row + CHUNK + 2].reshape((CHUNK + 2) * BCOLS, 1024),
            rest_w[n],
            preferred_element_type=F32,
        )
        size = CHUNK * BCOLS
        rest = (
            every[0:size, 0:64]
            + every[BCOLS : BCOLS + size, 64:128]
            + every[2 * BCOLS : 2 * BCOLS + size, 128:192]
        )
        bias = table[bias_at : bias_at + 1, :]
        return jnp.concatenate([main + bias[:, 0:256], rest + bias[:, 256:320]], axis=1)

    arrange(0)
    arrange(1)
    proj_load.wait()
    latent_load.wait()
    chalo.receive([cspread.at[0], cspread.at[1]], sides)
    branch_part(0, range(0, 8))
    branch_part(1, range(8, 16))
    bhalo.send()
    arrange(2)

    bhalo.receive([bspread], sides)
    for row in range(0, BROWS, CHUNK):
        value = swish(conv_base(2, bspread, row, BIAS + 3), table, SECOND)
        for k in range(CHUNK // 4):
            place(bimage, 0, row // 4 + k, value[k * BLOCK : (k + 1) * BLOCK])
            spread(
                bimage, 0, row // 4 + k, BCOLS, hspread.at[pl.ds(row + 4 * k + 1, 4)]
            )
    hhalo.send()

    branch_part(2)
    branch_part(3)
    arrange(3)

    hhalo.receive([hspread], sides)
    for row in range(0, BROWS, CHUNK):
        value = conv_base(3, hspread, row, BIAS + 4).reshape(CHUNK, BCOLS, C)
        outer[row : row + CHUNK] = value + latent[row : row + CHUNK].astype(F32)

    for step in range(3):
        for part in range(4):
            res_copy(step, part).wait_recv()

    def add_residual(n, _):
        rows = pl.ds(n * 4, 4)
        rest = got[n, 256:320]
        pieces = (
            got[n, 0:128],
            got[n, 128:256],
            jnp.concatenate([rest[:, 0:64], rest[:, 64:128]], axis=0),
        )
        for lanes, piece in zip((slice(0, 128), slice(128, 256), slice(256, 320)), pieces):
            total = outer[rows, :, lanes].reshape(BLOCK, -1) + piece.astype(F32)
            out_ref[rows, :, lanes] = total.astype(BF16).reshape(4, BCOLS, -1)
        return 0

    lax.fori_loop(0, BROWS // 4, add_residual, 0)
    for step in range(3):
        for part in range(4):
            res_copy(step, part).wait_send()
    for halo in (chalo, bhalo, hhalo):
        halo.finish()


def halo_scratch(planes, rows, cols):
    both = [
        pltpu.VMEM((2, planes, cols, 128), BF16),
        pltpu.VMEM((2, planes, rows, 128), BF16),
        pltpu.VMEM((4, planes, 16, 128), BF16),
    ]
    return both + both + [pltpu.SemaphoreType.DMA((8,)), pltpu.SemaphoreType.DMA((8,))]


def body(
    sizes,
    latent,
    control,
    first_mean,
    first_scale,
    first_gain,
    first_shift,
    first_kernel,
    first_bias,
    branch_mean,
    branch_scale,
    branch_gain,
    branch_shift,
    branch_kernel,
    branch_bias,
    proj_weight,
    proj_bias,
    second_mean,
    second_scale,
    second_gain,
    second_shift,
    second_kernel,
    second_bias,
):
    hbm = pl.BlockSpec(memory_space=pl.ANY)
    vmem = pl.BlockSpec(memory_space=pltpu.VMEM)
    return pl.pallas_call(
        functools.partial(kernel, sizes),
        out_shape=jax.ShapeDtypeStruct((BROWS, BCOLS, C), BF16),
        in_specs=[hbm] * 6 + [vmem] * 16,
        out_specs=vmem,
        scratch_shapes=[
            pltpu.VMEM((16, C), F32),
            pltpu.VMEM((BROWS, BCOLS, C), BF16),
            pltpu.VMEM((2, CROWS, C, CCOLS), BF16),
            pltpu.VMEM((4, 3, 3, 256, 256), BF16),
            pltpu.VMEM((4, 3, 4, 64, 256), BF16),
            pltpu.VMEM((4, 1024, 256), BF16),
            pltpu.VMEM((4, 3, 3, C, 64), BF16),
            pltpu.VMEM((2, C, C), BF16),
            pltpu.VMEM((6, CROWS + 1, STRIDE, 128), F32),
            pltpu.VMEM((3, BROWS // 4 + 1, STRIDE, 128), F32),
            pltpu.VMEM((2, CROWS + 2, CCOLS, 1024), BF16),
            pltpu.VMEM((BROWS + 2, BCOLS, 1024), BF16),
            pltpu.VMEM((BROWS + 2, BCOLS, 1024), BF16),
            pltpu.VMEM((2, CROWS + 2, CCOLS, 256), F32),
            pltpu.VMEM((BROWS, BCOLS, C), F32),
            pltpu.VMEM((4, 4, 320, 128), BF16),
            pltpu.VMEM((16, 320, 128), BF16),
            pltpu.VMEM((2, 3, BROWS // 8, 8, 128), F32),
        ]
        + halo_scratch(6, CROWS, CCOLS)
        + halo_scratch(3, BROWS, BCOLS)
        + halo_scratch(3, BROWS, BCOLS)
        + [
            pltpu.SemaphoreType.DMA((4,)),
            pltpu.SemaphoreType.DMA((4, 3)),
            pltpu.SemaphoreType.DMA((3, 4)),
            pltpu.SemaphoreType.DMA((3, 4)),
        ],
        compiler_params=pltpu.CompilerParams(
            collective_id=0, has_side_effects=True, vmem_limit_bytes=67_000_000
        ),
    )(
        latent,
        jnp.transpose(control, (0, 1, 3, 2)),
        first_kernel,
        branch_kernel,
        second_kernel,
        proj_weight,
        first_mean,
        first_scale,
        first_gain,
        first_shift,
        first_bias,
        branch_mean,
        branch_scale,
        branch_gain,
        branch_shift,
        branch_bias,
        proj_bias,
        second_mean,
        second_scale,
        second_gain,
        second_shift,
        second_bias,
    )


def solution(mesh):
    sizes = (mesh.shape["group"], mesh.shape["col"], mesh.shape["row"])
    in_specs = (
        P("group", ("col", "row"), None),
        P(None, ("group", "row"), "col", None),
    ) + (P(),) * 20
    out_specs = P("group", ("col", "row"), None)
    return jax.shard_map(
        functools.partial(body, sizes),
        mesh=mesh,
        in_specs=in_specs,
        out_specs=out_specs,
        check_vma=False,
    )
```

time: 77.4 us -> 59.9 us (0.77)
  the two profiles are of different devices: /device:TPU:14 before, /device:TPU:11 now
where the time goes in v1:
time: 59.9 us; the launch traced here: 59.6 us
  Pallas kernels  56.8 us (95%)
  local copies, waits for them, and re-layouts  2.71 us (5%)
    pallas_call x1, Pallas kernels, body(): pl.pallas_call(functools.partial(kernel, sizes), out_shape=jax.ShapeDtype...  56.8 us
    unnamed x1, local copies, waits for them, and re-layouts  2.71 us

profile of v1, /device:TPU:11, one launch (start us, length us, event | category | flops | bytes accessed | tf_op | source)
XLA Modules:
  0.0 59.6 jit_solution(9888634381713366443)
XLA Ops:
  0.0 56.8 %shard_map.208 = bf16[64,32,320]{2,1,0:T(8,128)(2,1)} custom-call(bf16[64,32,320]{2,1,0:T(8,128)(2,1)} %latent_hbm.1, bf16[2,16,320,128]{3,2,1,0:T(8,128)(2,1)} %bitcast.1, bf16[3,3,320,320]{3,2,1,0:T(8,128)(2,1)} %first_hbm.1, bf16[2,3,3,320,320]{4,3,2,1,0:T(8,128)(2,1)} %branch_hbm.1, bf16[3,3,320,320]{3,2,1,0:T(8,128)(2,1)} %second_hbm.1, ...), custom_call_target="tpu_custom_call" | custom-call | tf_op jit(solution)/shard_map/pallas_call | solution.py:560
  56.8 2.7 %copy.24 = bf16[64,32,320]{2,1,0:T(8,128)(2,1)} copy(bf16[64,32,320]{2,1,0:T(8,128)(2,1)} %shard_map.208) | data formatting | bytes 2621440

commit v2 on v1

--- a/solution.py
+++ b/solution.py
@@ -17,6 +17,7 @@
 BROWS, BCOLS = 64, 32
 BLOCK, STRIDE = 128, 144
 PART = 4
+VMEM_LIMIT = 57 * 2**20
 CHUNK = 16
 
 
@@ -65,7 +66,8 @@
 
 
 class Halo:
-    def __init__(self, tiling, image, rows, cols, bufs):
+    def __init__(self, tiling, image, rows, cols, bufs, raw=None):
+        self.raw = raw
         self.tiling, self.image, self.rows, self.cols = tiling, image, rows, cols
         self.srow, self.scol, self.scor, self.rrow, self.rcol, self.rcor, self.ss, self.rs = bufs
         self.planes = image.shape[0]
@@ -83,8 +85,12 @@
 
     def copy(self, i, j):
         n = DIRS.index((i, j))
+        if self.raw is not None and j == 0:
+            source = self.raw[0].at[:, 0 if i == -1 else self.rows - 1]
+        else:
+            source = self.slot(i, j, (self.srow, self.scol, self.scor))
         return pltpu.make_async_remote_copy(
-            src_ref=self.slot(i, j, (self.srow, self.scol, self.scor)),
+            src_ref=source,
             dst_ref=self.slot(i, j, (self.rrow, self.rcol, self.rcor)),
             send_sem=self.ss.at[n],
             recv_sem=self.rs.at[n],
@@ -94,11 +100,20 @@
 
     def clear(self):
         for i, j in DIRS:
+            if self.raw is not None and j == 0:
+                continue
 
             @pl.when(jnp.logical_not(self.tiling.has(-i, -j)))
             def _():
                 slot = self.slot(i, j, (self.rrow, self.rcol, self.rcor))
                 slot[...] = jnp.zeros(slot.shape, slot.dtype)
+
+    def start(self, dirs):
+        for i, j in dirs:
+
+            @pl.when(self.tiling.has(i, j))
+            def _():
+                self.copy(i, j).start()
 
     def send(self):
         cols, blocks = self.cols, self.blocks
@@ -106,7 +121,10 @@
         for p in range(self.planes):
             for i in (-1, 1):
                 block, at = edge[i]
-                self.srow[(i + 1) // 2, p] = self.image[p, block, at : at + cols, :].astype(BF16)
+                if self.raw is None:
+                    self.srow[(i + 1) // 2, p] = self.image[
+                        p, block, at : at + cols, :
+                    ].astype(BF16)
                 for j in (-1, 1):
                     pixel = at + (cols - 1) * ((j + 1) // 2)
                     self.scor[(i + 1) + (j + 1) // 2, p] = jnp.broadcast_to(
@@ -118,11 +136,7 @@
                     self.scol[(j + 1) // 2, p, inner * blocks : (inner + 1) * blocks] = self.flat[
                         p, pl.ds(start, blocks, stride=STRIDE), :
                     ].astype(BF16)
-        for i, j in DIRS:
-
-            @pl.when(self.tiling.has(i, j))
-            def _():
-                self.copy(i, j).start()
+        self.start([(i, j) for i, j in DIRS if self.raw is None or j != 0])
 
     def receive(self, targets, sides):
         cols, blocks = self.cols, self.blocks
@@ -134,9 +148,23 @@
 
         for n, target in enumerate(targets):
             for i in (-1, 1):
+                if self.raw is not None:
+                    here = self.tiling.has(-i, 0)
+
+                    @pl.when(here)
+                    def _():
+                        place(self.image, 3 * n, blocks, self.raw[1](self.rrow[(i + 1) // 2, n], n))
+
+                    @pl.when(jnp.logical_not(here))
+                    def _():
+                        place(self.image, 3 * n, blocks, jnp.zeros((BLOCK, C), F32))
+
                 for t in range(3):
                     p = 3 * n + t
-                    self.image[p, blocks, 8 : 8 + cols, :] = self.rrow[(i + 1) // 2, p].astype(F32)
+                    if self.raw is None:
+                        self.image[p, blocks, 8 : 8 + cols, :] = self.rrow[
+                            (i + 1) // 2, p
+                        ].astype(F32)
                     for j, at in ((1, 7), (-1, 8 + cols)):
                         self.image[p, blocks, at : at + 1, :] = self.rcor[
                             (i + 1) + (j + 1) // 2, p
@@ -232,14 +260,13 @@
     second_gain,
     second_shift,
     second_bias,
-    out_ref,
+    outer_hbm,
+    got,
     table,
     latent,
     control,
-    main_w,
-    tail_w,
+    all_w,
     rest_w,
-    stage_w,
     proj_w,
     cimage,
     bimage,
@@ -249,12 +276,11 @@
     crest,
     outer,
     send,
-    got,
     sides,
     *more,
 ):
     halo_bufs = [more[0:8], more[8:16], more[16:24]]
-    load_sem, weight_sem, res_send, res_recv = more[24:]
+    load_sem, weight_sem, res_send, res_recv, own_sem, outer_sem = more[24:]
     g, c, r = (lax.axis_index(a) for a in ("group", "col", "row"))
     nr = sizes[2]
     ctile, btile = Tiling(sizes, "branch"), Tiling(sizes, "base")
@@ -286,7 +312,10 @@
     for step in range(3):
         pl.semaphore_signal(barrier, inc=1, device_id=(g, c, peer(step)), device_id_type=MESH)
 
-    chalo = Halo(ctile, cimage, CROWS, CCOLS, halo_bufs[0])
+    def act_control(value, branch):
+        return swish(value.T.astype(F32), table, BRANCH + 2 * branch)
+
+    chalo = Halo(ctile, cimage, CROWS, CCOLS, halo_bufs[0], raw=(control, act_control))
     bhalo = Halo(btile, bimage, BROWS, BCOLS, halo_bufs[1])
     hhalo = Halo(btile, bimage, BROWS, BCOLS, halo_bufs[2])
 
@@ -314,37 +343,30 @@
 
     def weight_loads(n):
         ref = (branch_hbm.at[0], branch_hbm.at[1], first_hbm, second_hbm)[n]
-        return (
-            pltpu.make_async_copy(
-                ref.at[:, :, 0:256, 0:256], main_w.at[n], weight_sem.at[n, 0]
-            ),
-            pltpu.make_async_copy(
-                ref.at[:, :, 256:320, 0:256], tail_w.at[n, :, 0:3], weight_sem.at[n, 1]
-            ),
-            pltpu.make_async_copy(ref.at[:, :, :, 256:320], stage_w.at[n], weight_sem.at[n, 2]),
-        )
+        return (pltpu.make_async_copy(ref, all_w.at[n], weight_sem.at[n]),)
 
     for load in (
+        latent_load,
         *weight_loads(0),
         *weight_loads(1),
         proj_load,
-        latent_load,
         *weight_loads(2),
         *weight_loads(3),
     ):
         load.start()
 
+    pl.semaphore_wait(barrier, count)
+    chalo.start([(-1, 0), (1, 0)])
     for branch in range(2):
 
-        def act_control(n, _):
+        def control_rows(n, _):
             for row in (2 * n, 2 * n + 1):
-                value = swish(control[branch, row].T.astype(F32), table, BRANCH + 2 * branch)
+                value = act_control(control[branch, row], branch)
                 place(cimage, 3 * branch, row, value)
                 spread(cimage, 3 * branch, row, CCOLS, cspread.at[branch, pl.ds(row + 1, 1)])
             return 0
 
-        lax.fori_loop(0, CROWS // 2, act_control, 0)
-    pl.semaphore_wait(barrier, count)
+        lax.fori_loop(0, CROWS // 2, control_rows, 0)
     chalo.send()
     chalo.clear()
     bhalo.clear()
@@ -356,21 +378,21 @@
 
         def tap_column(dx, _):
             for at, start, size in ((dx * 256, 0, 256), (768 + dx * 64, 256, 64)):
-                pieces = [stage_w[n, dy, dx, start : start + size, :] for dy in range(3)]
+                pieces = [all_w[n, dy, dx, start : start + size, 256:320] for dy in range(3)]
                 rest_w[n, pl.ds(at, size), :] = jnp.concatenate(
                     pieces + [jnp.zeros((size, 64), BF16)], axis=1
                 )
             return 0
 
         lax.fori_loop(0, 3, tap_column, 0)
-        for dy in range(3):
-            tail_w[n, dy, 3] = jnp.zeros((64, 256), BF16)
         rest_w[n, 960:1024, :] = jnp.zeros((64, 256), BF16)
 
     def main_dot(image_rows, n):
         weight = []
         for dy in range(3):
-            weight += [main_w[n, dy].reshape(768, 256), tail_w[n, dy].reshape(256, 256)]
+            weight += [all_w[n, dy, dx, 0:256, 0:256] for dx in range(3)]
+            weight += [all_w[n, dy, dx, 256:320, 0:256] for dx in range(3)]
+            weight.append(jnp.zeros((64, 256), BF16))
         return jnp.dot(
             jnp.concatenate(image_rows, axis=1),
             jnp.concatenate(weight, axis=0),
@@ -395,13 +417,14 @@
             device_id_type=MESH,
         )
 
-    def branch_part(part, beside=()):
+    def own_copy(part):
+        return pltpu.make_async_copy(send.at[r, part], got.at[r * 4 + part], own_sem.at[part])
+
+    def branch_part(part):
         row = part * PART
         first, last = (0, PART + 2) if part == 0 else (row + 2, row + PART + 2)
         features = []
         for branch in range(2):
-            for work in beside[branch::2]:
-                act_latent(work)
             size = (last - first) * CCOLS
             crest[branch, first:last] = jnp.dot(
                 cspread[branch, first:last].reshape(size, 1024),
@@ -446,7 +469,7 @@
             ).astype(BF16)
         for step in range(3):
             res_copy(step, part).start()
-        got[r * 4 + part] = send[r, part]
+        own_copy(part).start()
 
     def conv_base(n, image, row, bias_at):
         main = main_dot(
@@ -467,14 +490,21 @@
         bias = table[bias_at : bias_at + 1, :]
         return jnp.concatenate([main + bias[:, 0:256], rest + bias[:, 256:320]], axis=1)
 
+    latent_load.wait()
+
+    def latent_blocks(n, _):
+        act_latent(2 * n)
+        act_latent(2 * n + 1)
+        return 0
+
+    lax.fori_loop(0, BROWS // 8, latent_blocks, 0)
+    bhalo.send()
     arrange(0)
     arrange(1)
     proj_load.wait()
-    latent_load.wait()
     chalo.receive([cspread.at[0], cspread.at[1]], sides)
-    branch_part(0, range(0, 8))
-    branch_part(1, range(8, 16))
-    bhalo.send()
+    branch_part(0)
+    branch_part(1)
     arrange(2)
 
     bhalo.receive([bspread], sides)
@@ -492,16 +522,31 @@
     arrange(3)
 
     hhalo.receive([hspread], sides)
+
+    def outer_copy(row):
+        rows = pl.ds(row, CHUNK)
+        return pltpu.make_async_copy(
+            outer.at[rows], outer_hbm.at[rows], outer_sem.at[row // CHUNK]
+        )
+
     for row in range(0, BROWS, CHUNK):
         value = conv_base(3, hspread, row, BIAS + 4).reshape(CHUNK, BCOLS, C)
         outer[row : row + CHUNK] = value + latent[row : row + CHUNK].astype(F32)
-
-    for step in range(3):
-        for part in range(4):
-            res_copy(step, part).wait_recv()
-
-    def add_residual(n, _):
-        rows = pl.ds(n * 4, 4)
+        outer_copy(row).start()
+
+    for part in range(4):
+        own_copy(part).wait()
+        for step in range(3):
+            res_copy(step, part).wait()
+    for row in range(0, BROWS, CHUNK):
+        outer_copy(row).wait()
+    for halo in (chalo, bhalo, hhalo):
+        halo.finish()
+
+
+def add_residual(outer, got, out):
+    for n in range(CHUNK // 4):
+        rows = slice(4 * n, 4 * n + 4)
         rest = got[n, 256:320]
         pieces = (
             got[n, 0:128],
@@ -510,24 +555,18 @@
         )
         for lanes, piece in zip((slice(0, 128), slice(128, 256), slice(256, 320)), pieces):
             total = outer[rows, :, lanes].reshape(BLOCK, -1) + piece.astype(F32)
-            out_ref[rows, :, lanes] = total.astype(BF16).reshape(4, BCOLS, -1)
-        return 0
-
-    lax.fori_loop(0, BROWS // 4, add_residual, 0)
-    for step in range(3):
-        for part in range(4):
-            res_copy(step, part).wait_send()
-    for halo in (chalo, bhalo, hhalo):
-        halo.finish()
-
-
-def halo_scratch(planes, rows, cols):
+            out[rows, :, lanes] = total.astype(BF16).reshape(4, BCOLS, -1)
+
+
+def halo_scratch(planes, rows, cols, raw=False):
+    row = pltpu.VMEM((2, 2, C, 128) if raw else (2, planes, cols, 128), BF16)
     both = [
-        pltpu.VMEM((2, planes, cols, 128), BF16),
+        row,
         pltpu.VMEM((2, planes, rows, 128), BF16),
         pltpu.VMEM((4, planes, 16, 128), BF16),
     ]
-    return both + both + [pltpu.SemaphoreType.DMA((8,)), pltpu.SemaphoreType.DMA((8,))]
+    send = [pltpu.VMEM((8, 128), BF16)] + both[1:] if raw else both
+    return send + both + [pltpu.SemaphoreType.DMA((8,)), pltpu.SemaphoreType.DMA((8,))]
 
 
 def body(
@@ -557,19 +596,20 @@
 ):
     hbm = pl.BlockSpec(memory_space=pl.ANY)
     vmem = pl.BlockSpec(memory_space=pltpu.VMEM)
-    return pl.pallas_call(
+    outer, residual = pl.pallas_call(
         functools.partial(kernel, sizes),
-        out_shape=jax.ShapeDtypeStruct((BROWS, BCOLS, C), BF16),
+        out_shape=(
+            jax.ShapeDtypeStruct((BROWS, BCOLS, C), F32),
+            jax.ShapeDtypeStruct((16, 320, 128), BF16),
+        ),
         in_specs=[hbm] * 6 + [vmem] * 16,
-        out_specs=vmem,
+        out_specs=(hbm, hbm),
         scratch_shapes=[
             pltpu.VMEM((16, C), F32),
             pltpu.VMEM((BROWS, BCOLS, C), BF16),
             pltpu.VMEM((2, CROWS, C, CCOLS), BF16),
-            pltpu.VMEM((4, 3, 3, 256, 256), BF16),
-            pltpu.VMEM((4, 3, 4, 64, 256), BF16),
+            pltpu.VMEM((4, 3, 3, C, C), BF16),
             pltpu.VMEM((4, 1024, 256), BF16),
-            pltpu.VMEM((4, 3, 3, C, 64), BF16),
             pltpu.VMEM((2, C, C), BF16),
             pltpu.VMEM((6, CROWS + 1, STRIDE, 128), F32),
             pltpu.VMEM((3, BROWS // 4 + 1, STRIDE, 128), F32),
@@ -579,20 +619,21 @@
             pltpu.VMEM((2, CROWS + 2, CCOLS, 256), F32),
             pltpu.VMEM((BROWS, BCOLS, C), F32),
             pltpu.VMEM((4, 4, 320, 128), BF16),
-            pltpu.VMEM((16, 320, 128), BF16),
             pltpu.VMEM((2, 3, BROWS // 8, 8, 128), F32),
         ]
-        + halo_scratch(6, CROWS, CCOLS)
+        + halo_scratch(6, CROWS, CCOLS, raw=True)
         + halo_scratch(3, BROWS, BCOLS)
         + halo_scratch(3, BROWS, BCOLS)
         + [
             pltpu.SemaphoreType.DMA((4,)),
-            pltpu.SemaphoreType.DMA((4, 3)),
+            pltpu.SemaphoreType.DMA((4,)),
             pltpu.SemaphoreType.DMA((3, 4)),
             pltpu.SemaphoreType.DMA((3, 4)),
+            pltpu.SemaphoreType.DMA((4,)),
+            pltpu.SemaphoreType.DMA((4,)),
         ],
         compiler_params=pltpu.CompilerParams(
-            collective_id=0, has_side_effects=True, vmem_limit_bytes=67_000_000
+            collective_id=0, has_side_effects=True, vmem_limit_bytes=VMEM_LIMIT
         ),
     )(
         latent,
@@ -618,6 +659,14 @@
         second_shift,
         second_bias,
     )
+    rows = pl.BlockSpec((CHUNK, BCOLS, C), lambda n: (n, 0, 0))
+    return pl.pallas_call(
+        add_residual,
+        grid=(BROWS // CHUNK,),
+        out_shape=jax.ShapeDtypeStruct((BROWS, BCOLS, C), BF16),
+        in_specs=[rows, pl.BlockSpec((4, 320, 128), lambda n: (n, 0, 0))],
+        out_specs=rows,
+    )(outer, residual)
 
 
 def solution(mesh):

time: 59.9 us -> 49.6 us (0.83)
  Pallas kernels: 56.8 us -> 49.4 us
  local copies, waits for them, and re-layouts: 2.71 us -> 0 us
    pallas_call x1 -> x2, Pallas kernels: 56.8 us -> 49.4 us  [the longest x1 45.2 us: body(): pl.pallas_call(functools.partial(kernel, sizes), out_shape=(jax.ShapeDtyp...]
    unnamed x1 -> x0, local copies, waits for them, and re-layouts: 2.71 us -> none
where the time goes in v2:
time: 49.6 us; the launch traced here: 49.4 us
  Pallas kernels  49.4 us (100%)
    pallas_call x1, Pallas kernels, body(): pl.pallas_call(functools.partial(kernel, sizes), out_shape=(jax.ShapeDtyp...  45.2 us
    pallas_call x1, Pallas kernels, body(): pl.pallas_call(add_residual, grid=(BROWS // CHUNK,), out_shape=jax.ShapeD...  4.18 us

profile of v2, /device:TPU:11, one launch (start us, length us, event | category | flops | bytes accessed | tf_op | source)
XLA Modules:
  0.0 49.4 jit_solution(6750091680181937550)
XLA Ops:
  0.0 45.2 %shard_map.208 = (f32[64,32,320]{2,1,0:T(8,128)}, bf16[16,320,128]{2,1,0:T(8,128)(2,1)}) custom-call(bf16[64,32,320]{2,1,0:T(8,128)(2,1)} %latent_hbm.1, bf16[2,16,320,128]{3,2,1,0:T(8,128)(2,1)} %bitcast.1, bf16[3,3,320,320]{3,2,1,0:T(8,128)(2,1)} %first_hbm.1, bf16[2,3,3,320,320]{4,3,2,1,0:T(8,128)(2,1)} %branch_hbm.1, ...), custom_call_target="tpu_custom_call" | custom-call | tf_op jit(solution)/shard_map/pallas_call | solution.py:599
  45.2 4.2 %shard_map.209 = bf16[64,32,320]{2,1,0:T(8,128)(2,1)} custom-call(f32[64,32,320]{2,1,0:T(8,128)} %get-tuple-element.7.outer, bf16[16,320,128]{2,1,0:T(8,128)(2,1)} %get-tuple-element.8.got), custom_call_target="tpu_custom_call" | custom-call | tf_op jit(solution)/shard_map/pallas_call | solution.py:663

commit v3 on v2

--- a/solution.py
+++ b/solution.py
@@ -17,7 +17,7 @@
 BROWS, BCOLS = 64, 32
 BLOCK, STRIDE = 128, 144
 PART = 4
-VMEM_LIMIT = 57 * 2**20
+VMEM_LIMIT = 56 * 2**20
 CHUNK = 16
 
 
@@ -260,7 +260,7 @@
     second_gain,
     second_shift,
     second_bias,
-    outer_hbm,
+    outer,
     got,
     table,
     latent,
@@ -274,13 +274,12 @@
     bspread,
     hspread,
     crest,
-    outer,
     send,
     sides,
     *more,
 ):
     halo_bufs = [more[0:8], more[8:16], more[16:24]]
-    load_sem, weight_sem, res_send, res_recv, own_sem, outer_sem = more[24:]
+    load_sem, weight_sem, res_send, res_recv, own_sem = more[24:]
     g, c, r = (lax.axis_index(a) for a in ("group", "col", "row"))
     nr = sizes[2]
     ctile, btile = Tiling(sizes, "branch"), Tiling(sizes, "base")
@@ -522,40 +521,38 @@
     arrange(3)
 
     hhalo.receive([hspread], sides)
-
-    def outer_copy(row):
-        rows = pl.ds(row, CHUNK)
-        return pltpu.make_async_copy(
-            outer.at[rows], outer_hbm.at[rows], outer_sem.at[row // CHUNK]
-        )
-
     for row in range(0, BROWS, CHUNK):
         value = conv_base(3, hspread, row, BIAS + 4).reshape(CHUNK, BCOLS, C)
         outer[row : row + CHUNK] = value + latent[row : row + CHUNK].astype(F32)
-        outer_copy(row).start()
 
     for part in range(4):
         own_copy(part).wait()
         for step in range(3):
             res_copy(step, part).wait()
-    for row in range(0, BROWS, CHUNK):
-        outer_copy(row).wait()
     for halo in (chalo, bhalo, hhalo):
         halo.finish()
 
 
-def add_residual(outer, got, out):
-    for n in range(CHUNK // 4):
-        rows = slice(4 * n, 4 * n + 4)
-        rest = got[n, 256:320]
-        pieces = (
-            got[n, 0:128],
-            got[n, 128:256],
-            jnp.concatenate([rest[:, 0:64], rest[:, 64:128]], axis=0),
-        )
-        for lanes, piece in zip((slice(0, 128), slice(128, 256), slice(256, 320)), pieces):
-            total = outer[rows, :, lanes].reshape(BLOCK, -1) + piece.astype(F32)
-            out[rows, :, lanes] = total.astype(BF16).reshape(4, BCOLS, -1)
+def add_residual(outer, got, out_hbm, out, sem):
+    def copy(n):
+        rows = pl.ds(n * CHUNK, CHUNK)
+        return pltpu.make_async_copy(out.at[rows], out_hbm.at[rows], sem.at[n])
+
+    for n in range(BROWS // CHUNK):
+        for k in range(n * CHUNK // 4, (n + 1) * CHUNK // 4):
+            rows = slice(4 * k, 4 * k + 4)
+            rest = got[k, 256:320]
+            pieces = (
+                got[k, 0:128],
+                got[k, 128:256],
+                jnp.concatenate([rest[:, 0:64], rest[:, 64:128]], axis=0),
+            )
+            for lanes, piece in zip((slice(0, 128), slice(128, 256), slice(256, 320)), pieces):
+                total = outer[rows, :, lanes].reshape(BLOCK, -1) + piece.astype(F32)
+                out[rows, :, lanes] = total.astype(BF16).reshape(4, BCOLS, -1)
+        copy(n).start()
+    for n in range(BROWS // CHUNK):
+        copy(n).wait()
 
 
 def halo_scratch(planes, rows, cols, raw=False):
@@ -599,11 +596,11 @@
     outer, residual = pl.pallas_call(
         functools.partial(kernel, sizes),
         out_shape=(
-            jax.ShapeDtypeStruct((BROWS, BCOLS, C), F32),
-            jax.ShapeDtypeStruct((16, 320, 128), BF16),
+            pltpu.VMEM((BROWS, BCOLS, C), F32),
+            pltpu.VMEM((16, 320, 128), BF16),
         ),
         in_specs=[hbm] * 6 + [vmem] * 16,
-        out_specs=(hbm, hbm),
+        out_specs=(vmem, vmem),
         scratch_shapes=[
             pltpu.VMEM((16, C), F32),
             pltpu.VMEM((BROWS, BCOLS, C), BF16),
@@ -617,7 +614,6 @@
             pltpu.VMEM((BROWS + 2, BCOLS, 1024), BF16),
             pltpu.VMEM((BROWS + 2, BCOLS, 1024), BF16),
             pltpu.VMEM((2, CROWS + 2, CCOLS, 256), F32),
-            pltpu.VMEM((BROWS, BCOLS, C), F32),
             pltpu.VMEM((4, 4, 320, 128), BF16),
             pltpu.VMEM((2, 3, BROWS // 8, 8, 128), F32),
         ]
@@ -629,7 +625,6 @@
             pltpu.SemaphoreType.DMA((4,)),
             pltpu.SemaphoreType.DMA((3, 4)),
             pltpu.SemaphoreType.DMA((3, 4)),
-            pltpu.SemaphoreType.DMA((4,)),
             pltpu.SemaphoreType.DMA((4,)),
         ],
         compiler_params=pltpu.CompilerParams(
@@ -659,13 +654,16 @@
         second_shift,
         second_bias,
     )
-    rows = pl.BlockSpec((CHUNK, BCOLS, C), lambda n: (n, 0, 0))
     return pl.pallas_call(
         add_residual,
-        grid=(BROWS // CHUNK,),
         out_shape=jax.ShapeDtypeStruct((BROWS, BCOLS, C), BF16),
-        in_specs=[rows, pl.BlockSpec((4, 320, 128), lambda n: (n, 0, 0))],
-        out_specs=rows,
+        in_specs=[vmem, vmem],
+        out_specs=hbm,
+        scratch_shapes=[
+            pltpu.VMEM((BROWS, BCOLS, C), BF16),
+            pltpu.SemaphoreType.DMA((BROWS // CHUNK,)),
+        ],
+        compiler_params=pltpu.CompilerParams(vmem_limit_bytes=16 * 2**20),
     )(outer, residual)
 
 

time: 49.6 us -> 46.1 us (0.929)
  Pallas kernels: 49.4 us -> 45.8 us
    pallas_call x2, Pallas kernels: 49.4 us -> 45.8 us  [the longest x1 44.5 us: body(): pl.pallas_call(functools.partial(kernel, sizes), out_shape=(pltpu.VMEM((B...]
where the time goes in v3:
time: 46.1 us; the launch traced here: 46 us
  Pallas kernels  45.8 us (99%)
    pallas_call x1, Pallas kernels, body(): pl.pallas_call(functools.partial(kernel, sizes), out_shape=(pltpu.VMEM((B...  44.5 us
    pallas_call x1, Pallas kernels, body(): pl.pallas_call(add_residual, out_shape=jax.ShapeDtypeStruct((BROWS, BCOLS...  1.31 us

profile of v3, /device:TPU:11, one launch (start us, length us, event | category | flops | bytes accessed | tf_op | source)
XLA Modules:
  0.0 46.0 jit_solution(17160002490635340476)
XLA Ops:
  0.0 44.5 %shard_map.208 = (f32[64,32,320]{2,1,0:T(8,128)S(1)}, bf16[16,320,128]{2,1,0:T(8,128)(2,1)S(1)}) custom-call(bf16[64,32,320]{2,1,0:T(8,128)(2,1)} %latent_hbm.1, bf16[2,16,320,128]{3,2,1,0:T(8,128)(2,1)} %bitcast.1, bf16[3,3,320,320]{3,2,1,0:T(8,128)(2,1)} %first_hbm.1, bf16[2,3,3,320,320]{4,3,2,1,0:T(8,128)(2,1)} %branch_hbm.1, ...), custom_call_target="tpu_custom_call" | custom-call | tf_op jit(solution)/shard_map/pallas_call | solution.py:596
  44.5 1.3 %shard_map.209 = bf16[64,32,320]{2,1,0:T(8,128)(2,1)} custom-call(f32[64,32,320]{2,1,0:T(8,128)S(1)} %get-tuple-element.7.outer, bf16[16,320,128]{2,1,0:T(8,128)(2,1)S(1)} %get-tuple-element.8.got), custom_call_target="tpu_custom_call" | custom-call | tf_op jit(solution)/shard_map/pallas_call | solution.py:657

commit v4 on v3

--- a/solution.py
+++ b/solution.py
@@ -359,13 +359,13 @@
     for branch in range(2):
 
         def control_rows(n, _):
-            for row in (2 * n, 2 * n + 1):
+            for row in (4 * n, 4 * n + 1, 4 * n + 2, 4 * n + 3):
                 value = act_control(control[branch, row], branch)
                 place(cimage, 3 * branch, row, value)
                 spread(cimage, 3 * branch, row, CCOLS, cspread.at[branch, pl.ds(row + 1, 1)])
             return 0
 
-        lax.fori_loop(0, CROWS // 2, control_rows, 0)
+        lax.fori_loop(0, CROWS // 4, control_rows, 0)
     chalo.send()
     chalo.clear()
     bhalo.clear()

time: 46.1 us -> 46.1 us (level)
  no operation moved by 1% of the time
where the time goes in v4:
time: 46.1 us; the launch traced here: 45.9 us
  Pallas kernels  45.7 us (99%)
    pallas_call x1, Pallas kernels, body(): pl.pallas_call(functools.partial(kernel, sizes), out_shape=(pltpu.VMEM((B...  44.4 us
    pallas_call x1, Pallas kernels, body(): pl.pallas_call(add_residual, out_shape=jax.ShapeDtypeStruct((BROWS, BCOLS...  1.31 us

profile of v4, /device:TPU:11, one launch (start us, length us, event | category | flops | bytes accessed | tf_op | source)
XLA Modules:
  0.0 45.9 jit_solution(15288630658370943898)
XLA Ops:
  0.0 44.4 %shard_map.208 = (f32[64,32,320]{2,1,0:T(8,128)S(1)}, bf16[16,320,128]{2,1,0:T(8,128)(2,1)S(1)}) custom-call(bf16[64,32,320]{2,1,0:T(8,128)(2,1)} %latent_hbm.1, bf16[2,16,320,128]{3,2,1,0:T(8,128)(2,1)} %bitcast.1, bf16[3,3,320,320]{3,2,1,0:T(8,128)(2,1)} %first_hbm.1, bf16[2,3,3,320,320]{4,3,2,1,0:T(8,128)(2,1)} %branch_hbm.1, ...), custom_call_target="tpu_custom_call" | custom-call | tf_op jit(solution)/shard_map/pallas_call | solution.py:596
  44.4 1.3 %shard_map.209 = bf16[64,32,320]{2,1,0:T(8,128)(2,1)} custom-call(f32[64,32,320]{2,1,0:T(8,128)S(1)} %get-tuple-element.7.outer, bf16[16,320,128]{2,1,0:T(8,128)(2,1)S(1)} %get-tuple-element.8.got), custom_call_target="tpu_custom_call" | custom-call | tf_op jit(solution)/shard_map/pallas_call | solution.py:657
